TPU v7x, 32 devices: a whole 2x2x4 slice. The times are simulated.
32 devices in a mesh: expert: 4 (over z), tensor: 8 (over y, x, core).
Axes of the slice: x: 2, y: 2, z: 4, core: 2. Of those that a mesh axis runs over, the one named last changes fastest.
Arguments:
- tokens: bfloat16 [512, 6144], P('expert', 'tensor'), may hold values from -6 to 6
- out_grad: bfloat16 [512, 6144], P('expert', 'tensor'), may hold values from -6 to 6
- expert_ids: int32 [512, 2], P('expert'), may hold values from 0 to 3, all different within a row; in each aligned block of 128 rows (0 to 127, 128 to 255, ...) at most 80 rows name the same one
- route_logits: float32 [512, 2], P('expert'), may hold values from -6 to 6
- w_gate: bfloat16 [4, 6144, 8192], P('expert', 'tensor'), may hold values from -0.078125 to 0.078125
- w_up: bfloat16 [4, 6144, 8192], P('expert', 'tensor'), may hold values from -0.078125 to 0.078125
- w_down: bfloat16 [4, 6144, 8192], P('expert', 'tensor'), may hold values from -0.0625 to 0.0625
- gate_scale: float32 [4, 8192], P('expert', 'tensor'), may hold values from 0.5 to 2
- up_scale: float32 [4, 8192], P('expert', 'tensor'), may hold values from 0.5 to 2
- down_scale: float32 [4, 8192], P('expert', 'tensor'), may hold values from 0.5 to 2
Outputs:
- mixed: bfloat16 [512, 6144], P('expert', 'tensor')
- token_grad: bfloat16 [512, 6144], P('expert', 'tensor')
- logit_grad: float32 [512, 2], P('expert')
- gate_grad: bfloat16 [4, 6144, 8192], P('expert', None, 'tensor')
- up_grad: bfloat16 [4, 6144, 8192], P('expert', None, 'tensor')
- down_grad: bfloat16 [4, 6144, 8192], P('expert', None, 'tensor')
Inputs may be any that keep to these rules, and one draw needn't show every extreme that they name: `expert_ids`: each token names two different experts; among the 128 tokens of one index of the expert axis, each expert is named by at most 80.
All inputs are finite; a program needn't handle non-finite values.
Results may differ from a plain program's by a relative error of at most 0.025.
Values may be sent and summed in bfloat16 or wider, within the bound.
A program may use at most 256 MiB of HBM per device.

v0:
```python
import jax
import jax.numpy as jnp
from jax import lax
from jax.sharding import PartitionSpec as P


def gate_tables(expert_ids, route_logits, count):
    first = jax.nn.sigmoid(route_logits[:, 0] - route_logits[:, 1])
    probs = jnp.stack([first, 1.0 - first], axis=1)
    labels = jnp.arange(count, dtype=jnp.int32)
    chosen = (expert_ids[:, :, None] == labels[None, None, :]).astype(jnp.float32)
    per_expert = jnp.sum(probs[:, :, None] * chosen, axis=1)
    member = jnp.sum(chosen, axis=1)
    return (probs, chosen, per_expert, member)


def contract_rows(left, right):
    return lax.dot_general(
        left, right, (((0,), (0,)), ((), ())), preferred_element_type=jnp.float32
    )


def body(
    tokens,
    out_grad,
    expert_ids,
    route_logits,
    w_gate,
    w_up,
    w_down,
    gate_scale,
    up_scale,
    down_scale,
):
    groups = lax.axis_size("expert")
    local_tokens, feat_width = tokens.shape
    cap = local_tokens * 5 // 8
    total_rows = groups * cap
    probs, chosen, per_expert, member = gate_tables(expert_ids, route_logits, groups)
    weight_cols = per_expert.T[:, :, None]
    earlier = jnp.tril(jnp.ones((local_tokens, local_tokens), jnp.bfloat16), -1)
    rank = jnp.dot(earlier, member.astype(jnp.bfloat16), preferred_element_type=jnp.float32)
    slots = jnp.arange(cap, dtype=jnp.float32)
    place = jnp.where(
        (member.T[:, None, :] > 0) & (rank.T[:, None, :] == slots[None, :, None]), 1.0, 0.0
    ).astype(jnp.bfloat16)
    weighted = (out_grad.astype(jnp.float32)[None] * weight_cols).astype(jnp.bfloat16)
    send_rows = jnp.einsum("eit,td->eid", place, tokens, preferred_element_type=jnp.float32)
    send_grads = jnp.einsum("eit,etd->eid", place, weighted, preferred_element_type=jnp.float32)
    send = jnp.stack([send_rows, send_grads], axis=1).astype(jnp.bfloat16)
    got = lax.all_to_all(send, "expert", split_axis=0, concat_axis=0, tiled=True)
    rows_loc = got[:, 0].reshape(total_rows, feat_width)
    grads_loc = got[:, 1].reshape(total_rows, feat_width)
    gate_w, up_w, down_w = (w_gate[0], w_up[0], w_down[0])

    def project(left, right):
        part = jnp.dot(left, right, preferred_element_type=jnp.float32).astype(jnp.bfloat16)
        full = lax.psum_scatter(part, "tensor", scatter_dimension=1, tiled=True)
        return full.astype(jnp.float32)

    def gather(value):
        return lax.all_gather(value, "tensor", axis=1, tiled=True)

    def back_project(left, right):
        return lax.dot_general(
            left, right, (((1,), (1,)), ((), ())), preferred_element_type=jnp.float32
        )

    def send_back(value):
        return lax.all_to_all(
            value.astype(jnp.bfloat16).reshape(groups, cap, feat_width),
            "expert",
            split_axis=0,
            concat_axis=0,
            tiled=True,
        )

    gate_pre = project(rows_loc, gate_w) * gate_scale[0]
    up_pre = project(rows_loc, up_w) * up_scale[0]
    back = project(grads_loc, down_w) * down_scale[0]
    rows_in = gather(rows_loc)
    grads_in = gather(grads_loc)
    sigma = jax.nn.sigmoid(gate_pre)
    active = gate_pre * sigma
    hidden = (active * up_pre * down_scale[0]).astype(jnp.bfloat16)
    d_gate = (back * up_pre * sigma * (1.0 + gate_pre * (1.0 - sigma)) * gate_scale[0]).astype(
        jnp.bfloat16
    )
    d_up = (back * active * up_scale[0]).astype(jnp.bfloat16)
    out_back = send_back(back_project(gather(hidden), down_w))
    grad_back = send_back(back_project(gather(d_gate), gate_w) + back_project(gather(d_up), up_w))
    down_grad = contract_rows(grads_in, hidden).astype(jnp.bfloat16)
    gate_grad = contract_rows(rows_in, d_gate).astype(jnp.bfloat16)
    up_grad = contract_rows(rows_in, d_up).astype(jnp.bfloat16)
    out_float = jnp.einsum("eit,eid->etd", place, out_back, preferred_element_type=jnp.float32)
    token_grad = lax.dot_general(
        place.reshape(total_rows, local_tokens),
        grad_back.reshape(total_rows, feat_width),
        (((0,), (0,)), ((), ())),
        preferred_element_type=jnp.float32,
    ).astype(jnp.bfloat16)
    mixed = jnp.sum(weight_cols * out_float, axis=0).astype(jnp.bfloat16)
    local_score = jnp.einsum("td,etd->te", out_grad.astype(jnp.float32), out_float)
    score = lax.psum(local_score, "tensor")
    pick = jnp.sum(chosen * score[:, None, :], axis=2)
    mean_pick = jnp.sum(probs * pick, axis=1, keepdims=True)
    logit_grad = probs * (pick - mean_pick)
    return (mixed, token_grad, logit_grad, gate_grad[None], up_grad[None], down_grad[None])


def solution(mesh):
    in_specs = (
        P("expert", "tensor"),
        P("expert", "tensor"),
        P("expert", None),
        P("expert", None),
        P("expert", "tensor", None),
        P("expert", "tensor", None),
        P("expert", "tensor", None),
        P("expert", "tensor"),
        P("expert", "tensor"),
        P("expert", "tensor"),
    )
    out_specs = (
        P("expert", "tensor"),
        P("expert", "tensor"),
        P("expert", None),
        P("expert", None, "tensor"),
        P("expert", None, "tensor"),
        P("expert", None, "tensor"),
    )
    return jax.shard_map(body, mesh=mesh, in_specs=in_specs, out_specs=out_specs, check_vma=False)
```

profile of v0, /device:TPU:0, one launch (start us, length us, event | category | flops | bytes accessed | tf_op | source)
XLA Modules:
  0.0 471.8 jit_solution(13692234341856689508)
XLA Ops:
  7.2 0.0 copy-start
  7.2 0.0 reduce-scatter.8.cloned.1.call-start
  7.2 0.8 broadcast_subtract_fusion
  8.0 0.7 convert_reduce_fusion
  8.7 0.2 fusion.59
  8.9 1.0 convert_element_type.68
  9.9 0.0 copy-done
  9.9 0.3 fusion.33
  10.2 0.4 fusion.34
  10.6 0.1 pad_maximum_fusion
  10.7 0.1 copy.21
  10.7 30.5 %all_to_all.15 = bf16[4,2,80,768]{3,2,1,0:T(8,128)(2,1)S(1)} all-to-all(bf16[4,2,80,768]{3,2,1,0:T(8,128)(2,1)S(1)} %copy.21), channel_id=1, replica_groups=mesh['expert'=4,'tensor'=8] {'expert'}, dimensions={0} | all-to-all | bytes 1966080 | tf_op jit(solution)/shard_map/all_to_all | solution.py:51
  41.2 0.1 fusion.75
  41.3 0.0 copy-start.4
  41.3 0.0 copy-start.5
  41.3 10.9 %fusion.18 = bf16[320,8192]{1,0:T(8,128)(2,1)} fusion(bf16[320,768]{1,0:T(8,128)(2,1)S(1)} %bitcast.70, bf16[1,768,8192]{2,1,0:T(8,128)(2,1)} %param.16), kind=kOutput, calls=%fused_computation.17 | convolution fusion | flops 4029153280 | bytes 18317312 | tf_op jit(solution)/shard_map/dot_general | solution.py:57
  52.2 0.0 copy-done.4
  52.2 0.0 reduce-scatter.8.cloned.1.call-update
  52.3 0.0 reduce-scatter.6.cloned.1.call-start
  52.3 10.6 %fusion.15 = bf16[320,8192]{1,0:T(8,128)(2,1)} fusion(bf16[320,768]{1,0:T(8,128)(2,1)S(1)} %bitcast.72, bf16[1,768,8192]{2,1,0:T(8,128)(2,1)} %param.15), kind=kOutput, calls=%fused_computation.16 | convolution fusion | flops 4029153280 | bytes 18317312 | tf_op jit(solution)/shard_map/dot_general | solution.py:57
  62.9 0.0 reduce-scatter.6.cloned.1.call-update
  63.0 0.0 reduce-scatter.4.cloned.1.call-start
  63.0 0.0 copy-done.5
  63.0 11.2 %fusion.12 = bf16[320,8192]{1,0:T(8,128)(2,1)} fusion(bf16[320,768]{1,0:T(8,128)(2,1)S(1)} %bitcast.73, bf16[1,768,8192]{2,1,0:T(8,128)(2,1)} %param.14), kind=kOutput, calls=%fused_computation.15 | convolution fusion | flops 4029153280 | bytes 18317312 | tf_op jit(solution)/shard_map/dot_general | solution.py:57
  74.3 0.0 reduce-scatter.4.cloned.1.call-update
  74.3 0.0 all-gather.12.cloned.1.call-start
  74.3 0.5 all-gather.12.cloned.1.call-update
  74.9 0.0 all-gather.14.cloned.1.call-start
  74.9 0.5 all-gather.14.cloned.1.call-update
  75.4 0.0 all-gather.6.cloned.1.call-start
  75.5 32.4 %reduce-scatter.8.cloned.1.call-done = bf16[320,1024]{1,0:T(8,128)(2,1)} async-done(((bf16[320,8192]{1,0:T(8,128)(2,1)}), bf16[320,1024]{1,0:T(8,128)(2,1)}) %reduce-scatter.8.cloned.1.call-update) | async-done | bytes 655376 | tf_op jit(solution)/shard_map/reduce_scatter | solution.py:58
  107.9 60.4 %reduce-scatter.6.cloned.1.call-done = bf16[320,1024]{1,0:T(8,128)(2,1)} async-done(((bf16[320,8192]{1,0:T(8,128)(2,1)}), bf16[320,1024]{1,0:T(8,128)(2,1)}) %reduce-scatter.6.cloned.1.call-update) | async-done | bytes 655376 | tf_op jit(solution)/shard_map/reduce_scatter | solution.py:58
  168.3 60.4 %reduce-scatter.4.cloned.1.call-done = bf16[320,1024]{1,0:T(8,128)(2,1)} async-done(((bf16[320,8192]{1,0:T(8,128)(2,1)}), bf16[320,1024]{1,0:T(8,128)(2,1)}) %reduce-scatter.4.cloned.1.call-update) | async-done | bytes 655376 | tf_op jit(solution)/shard_map/reduce_scatter | solution.py:58
  228.7 0.0 copy-done.7
  228.7 3.6 multiply_convert_fusion.2
  232.3 0.0 all-gather.6.cloned.1.call-update
  232.4 0.0 all-gather.10.cloned.1.call-start
  232.4 0.7 all-gather.10.cloned.1.call-update
  233.1 0.2 all-gather.8.cloned.1.call-start
  233.3 0.5 all-gather.8.cloned.1.call-update
  233.9 0.0 copy-start.2
  233.9 32.0 %all-gather.12.cloned.1.call-done = bf16[320,6144]{1,0:T(8,128)(2,1)} async-done(((bf16[320,768]{1,0:T(8,128)(2,1)}), bf16[320,6144]{1,0:T(8,128)(2,1)}) %all-gather.12.cloned.1.call-update) | async-done | bytes 3932176 | tf_op jit(solution)/shard_map/all_gather | solution.py:62
  265.9 12.1 %convert_bitcast_fusion.2 = bf16[1,6144,1024]{2,1,0:T(8,128)(2,1)} fusion(bf16[320,6144]{1,0:T(8,128)(2,1)} %all-gather.12.cloned.1.call-done, bf16[320,1024]{1,0:T(8,128)(2,1)} %get-tuple-element.10), kind=kOutput, calls=%fused_computation.14 | convolution fusion | flops 4032823296 | bytes 17170432 | tf_op jit(solution)/shard_map/dot_general | solution.py:18
  278.0 0.0 copy-done.11
  278.0 9.7 %convert_bitcast_fusion.1 = bf16[1,6144,1024]{2,1,0:T(8,128)(2,1)} fusion(bf16[320,6144]{1,0:T(8,128)(2,1)S(1)} %copy-done.11, bf16[320,1024]{1,0:T(8,128)(2,1)S(1)} %copy-done.2), kind=kOutput, calls=%fused_computation.13 | convolution fusion | flops 4032823296 | bytes 17170432 | tf_op jit(solution)/shard_map/dot_general | solution.py:18
  287.7 15.4 %all-gather.14.cloned.1.call-done = bf16[320,6144]{1,0:T(8,128)(2,1)} async-done(((bf16[320,768]{1,0:T(8,128)(2,1)}), bf16[320,6144]{1,0:T(8,128)(2,1)}) %all-gather.14.cloned.1.call-update) | async-done | bytes 3932176 | tf_op jit(solution)/shard_map/all_gather | solution.py:62
  303.1 11.8 %convert_bitcast_fusion = bf16[1,6144,1024]{2,1,0:T(8,128)(2,1)} fusion(bf16[320,6144]{1,0:T(8,128)(2,1)} %all-gather.14.cloned.1.call-done, bf16[320,1024]{1,0:T(8,128)(2,1)S(1)} %copy-done.3), kind=kOutput, calls=%fused_computation.12 | convolution fusion | flops 4032823296 | bytes 17170432 | tf_op jit(solution)/shard_map/dot_general | solution.py:18
  314.9 31.0 %all-gather.6.cloned.1.call-done = bf16[320,8192]{1,0:T(8,128)(2,1)} async-done(((bf16[320,1024]{1,0:T(8,128)(2,1)}), bf16[320,8192]{1,0:T(8,128)(2,1)}) %all-gather.6.cloned.1.call-update) | async-done | bytes 5242896 | tf_op jit(solution)/shard_map/all_gather | solution.py:62
  345.9 11.2 %fusion.30 = bf16[320,768]{1,0:T(8,128)(2,1)} fusion(bf16[320,8192]{1,0:T(8,128)(2,1)} %all-gather.6.cloned.1.call-done, bf16[1,768,8192]{2,1,0:T(8,128)(2,1)} %param.16), kind=kOutput, calls=%fused_computation.32 | convolution fusion | flops 4026777600 | bytes 18317312 | tf_op jit(solution)/shard_map/dot_general | solution.py:65
  357.1 4.6 all-to-all-start.1
  361.7 27.1 %all-gather.10.cloned.1.call-done = bf16[320,8192]{1,0:T(8,128)(2,1)} async-done(((bf16[320,1024]{1,0:T(8,128)(2,1)}), bf16[320,8192]{1,0:T(8,128)(2,1)}) %all-gather.10.cloned.1.call-update) | async-done | bytes 5242896 | tf_op jit(solution)/shard_map/all_gather | solution.py:62
  388.8 9.1 %fusion.4 = f32[320,768]{1,0:T(8,128)S(1)} fusion(bf16[320,8192]{1,0:T(8,128)(2,1)} %all-gather.10.cloned.1.call-done, bf16[1,768,8192]{2,1,0:T(8,128)(2,1)} %param.15), kind=kOutput, calls=%fused_computation.4 | convolution fusion | flops 4026531840 | bytes 18808832 | tf_op jit(solution)/shard_map/dot_general | solution.py:65
  397.9 0.0 copy-start.6
  397.9 33.8 %all-gather.8.cloned.1.call-done = bf16[320,8192]{1,0:T(8,128)(2,1)} async-done(((bf16[320,1024]{1,0:T(8,128)(2,1)}), bf16[320,8192]{1,0:T(8,128)(2,1)}) %all-gather.8.cloned.1.call-update) | async-done | bytes 5242896 | tf_op jit(solution)/shard_map/all_gather | solution.py:62
  431.7 11.3 %fusion.27 = bf16[320,768]{1,0:T(8,128)(2,1)} fusion(f32[320,768]{1,0:T(8,128)S(1)} %fusion.4, bf16[320,8192]{1,0:T(8,128)(2,1)} %all-gather.8.cloned.1.call-done, bf16[1,768,8192]{2,1,0:T(8,128)(2,1)} %param.14), kind=kOutput, calls=%fused_computation.31 | convolution fusion | flops 4027023360 | bytes 19300352 | tf_op jit(solution)/shard_map/dot_general | solution.py:65
  443.0 0.0 all-to-all-done.1
  443.0 4.7 %all-to-all-start.2 = ((bf16[4,80,768]{2,1,0:T(8,128)(2,1)}), bf16[4,80,768]{2,1,0:T(8,128)(2,1)S(1)}, u32[]{:S(2)}, u32[]{:S(2)}) async-start(bf16[4,80,768]{2,1,0:T(8,128)(2,1)} %bitcast.14), calls=%async_computation.5 | async-start | bytes 983040 | tf_op jit(solution)/shard_map/all_to_all | solution.py:70
  447.7 1.1 multiply_reduce_fusion
  448.8 1.1 fusion.21
  449.9 0.1 copy.24
  449.9 13.4 %psum.7 = f32[128,4]{0,1:T(4,128)S(1)} all-reduce(f32[128,4]{0,1:T(4,128)S(1)} %bitcast.78), channel_id=1, replica_groups=mesh['expert'=4,'tensor'=8] {'tensor'}, use_global_device_ids=true, to_apply=%region_6.7 | all-reduce | flops 512 | bytes 4096 | tf_op jit(solution)/shard_map/psum | solution.py:104
  463.4 0.6 subtract_multiply_fusion
  464.0 0.0 all-to-all-done.2
  464.0 1.0 fusion.35
  (19 shorter events, 0.1 us)
Async XLA Ops:
  7.2 2.7 copy-start
  7.2 100.7 %reduce-scatter.8.cloned.1.call-start = ((), (), s32[]{:S(2)}) async-start(), calls=%async_computation.9 | async-start | bytes 5898240 | tf_op jit(solution)/shard_map/reduce_scatter | solution.py:58
  41.3 11.0 %copy-start.4 = (bf16[4,1,80,768]{3,2,1,0:T(8,128)(2,1)}, bf16[4,1,80,768]{3,2,1,0:T(8,128)(2,1)S(1)}, u32[]{:S(2)}) copy-start(bf16[4,1,80,768]{3,2,1,0:T(8,128)(2,1)S(1)} %get-tuple-element.13) | copy-start | bytes 1474564
  41.3 21.7 %copy-start.5 = (bf16[4,1,80,768]{3,2,1,0:T(8,128)(2,1)}, bf16[4,1,80,768]{3,2,1,0:T(8,128)(2,1)S(1)}, u32[]{:S(2)}) copy-start(bf16[4,1,80,768]{3,2,1,0:T(8,128)(2,1)S(1)} %get-tuple-element.14) | copy-start | bytes 1474564
  52.3 116.0 %reduce-scatter.6.cloned.1.call-start = ((), (), s32[]{:S(2)}) async-start(), calls=%async_computation.7 | async-start | bytes 5898240 | tf_op jit(solution)/shard_map/reduce_scatter | solution.py:58
  63.0 165.7 %reduce-scatter.4.cloned.1.call-start = ((), (), s32[]{:S(2)}) async-start(), calls=%async_computation.6 | async-start | bytes 5898240 | tf_op jit(solution)/shard_map/reduce_scatter | solution.py:58
  74.2 154.5 %copy-start.7 = (f32[1,1024]{1,0:T(1,128)S(1)}, f32[1,1024]{1,0:T(1,128)}, u32[]{:S(2)}) copy-start(f32[1,1024]{1,0:T(1,128)} %param.19) | copy-start | bytes 12292
  74.2 154.5 %copy-start.8 = (f32[1,1024]{1,0:T(1,128)S(1)}, f32[1,1024]{1,0:T(1,128)}, u32[]{:S(2)}) copy-start(f32[1,1024]{1,0:T(1,128)} %param.18) | copy-start | bytes 12292
  74.3 154.5 %copy-start.9 = (f32[1,1024]{1,0:T(1,128)S(1)}, f32[1,1024]{1,0:T(1,128)}, u32[]{:S(2)}) copy-start(f32[1,1024]{1,0:T(1,128)} %param.17) | copy-start | bytes 12292
  74.3 191.6 %all-gather.12.cloned.1.call-start = ((), (), s32[]{:S(2)}) async-start(), calls=%async_computation.12 | async-start | bytes 4423680 | tf_op jit(solution)/shard_map/all_gather | solution.py:62
  74.9 228.2 %all-gather.14.cloned.1.call-start = ((), (), s32[]{:S(2)}) async-start(), calls=%async_computation.13 | async-start | bytes 4423680 | tf_op jit(solution)/shard_map/all_gather | solution.py:62
  75.4 270.4 %all-gather.6.cloned.1.call-start = ((), (), s32[]{:S(2)}) async-start(), calls=%async_computation.8 | async-start | bytes 5898240 | tf_op jit(solution)/shard_map/all_gather | solution.py:62
  232.4 156.4 %all-gather.10.cloned.1.call-start = ((), (), s32[]{:S(2)}) async-start(), calls=%async_computation.11 | async-start | bytes 5898240 | tf_op jit(solution)/shard_map/all_gather | solution.py:62
  233.1 198.6 %all-gather.8.cloned.1.call-start = ((), (), s32[]{:S(2)}) async-start(), calls=%async_computation.10 | async-start | bytes 5898240 | tf_op jit(solution)/shard_map/all_gather | solution.py:62
  233.9 44.1 %copy-start.2 = (bf16[320,1024]{1,0:T(8,128)(2,1)S(1)}, bf16[320,1024]{1,0:T(8,128)(2,1)}, u32[]{:S(2)}) copy-start(bf16[320,1024]{1,0:T(8,128)(2,1)} %get-tuple-element.12) | copy-start | bytes 1966084
  265.9 12.1 %copy-start.11 = (bf16[320,6144]{1,0:T(8,128)(2,1)S(1)}, bf16[320,6144]{1,0:T(8,128)(2,1)}, u32[]{:S(2)}) copy-start(bf16[320,6144]{1,0:T(8,128)(2,1)} %all-gather.12.cloned.1.call-done) | copy-start | bytes 11796484
  278.0 25.1 %copy-start.3 = (bf16[320,1024]{1,0:T(8,128)(2,1)S(1)}, bf16[320,1024]{1,0:T(8,128)(2,1)}, u32[]{:S(2)}) copy-start(bf16[320,1024]{1,0:T(8,128)(2,1)} %get-tuple-element.11) | copy-start | bytes 1966084
  357.1 85.9 %all-to-all-start.1 = ((bf16[4,80,768]{2,1,0:T(8,128)(2,1)}), bf16[4,80,768]{2,1,0:T(8,128)(2,1)S(1)}, u32[]{:S(2)}, u32[]{:S(2)}) async-start(bf16[4,80,768]{2,1,0:T(8,128)(2,1)} %bitcast.12), calls=%async_computation.3 | async-start | bytes 983040 | tf_op jit(solution)/shard_map/all_to_all | solution.py:70
  397.9 50.9 %copy-start.6 = (bf16[128,768]{1,0:T(8,128)(2,1)S(1)}, bf16[128,768]{1,0:T(8,128)(2,1)}, u32[]{:S(2)}) copy-start(bf16[128,768]{1,0:T(8,128)(2,1)} %param.11) | copy-start | bytes 589828
  431.7 33.3 %copy-start.1 = (bf16[128,768]{1,0:T(8,128)(2,1)S(1)}, bf16[128,768]{1,0:T(8,128)(2,1)}, u32[]{:S(2)}) copy-start(bf16[128,768]{1,0:T(8,128)(2,1)} %param.10) | copy-start | bytes 589828
  443.0 20.4 %copy-start.10 = (s32[128,2]{0,1:T(2,128)S(1)}, s32[128,2]{0,1:T(2,128)}, u32[]{:S(2)}) copy-start(s32[128,2]{0,1:T(2,128)} %param.12) | copy-start | bytes 3076
  443.0 21.0 %all-to-all-start.2 = ((bf16[4,80,768]{2,1,0:T(8,128)(2,1)}), bf16[4,80,768]{2,1,0:T(8,128)(2,1)S(1)}, u32[]{:S(2)}, u32[]{:S(2)}) async-start(bf16[4,80,768]{2,1,0:T(8,128)(2,1)} %bitcast.14), calls=%async_computation.5 | async-start | bytes 983040 | tf_op jit(solution)/shard_map/all_to_all | solution.py:70
Sparse Core Ops, SparseCore 0:
  52.4 55.4 reduce-scatter.7
  111.9 56.3 reduce-scatter.5
  172.3 56.3 reduce-scatter.3
  230.5 35.4 all-gather.11
  267.7 35.3 all-gather.13
  304.9 40.9 all-gather.5
  347.8 40.9 all-gather.9
  390.7 40.9 all-gather.7
where the time goes:
time: 472 us
  waiting for transfers between devices  295 us (62%)
  matrix products  102 us (22%)
  blocking collectives  43.9 us (9%)
  between operations  14.3 us (3%)
  starting transfers between devices  9.82 us (2%)
  other arithmetic  6.8 us (1%)
    reduce_scatter x3, waiting for transfers between devices, project(): full = lax.psum_scatter(part, 'tensor', scatter_dimension=1, tiled=True)  153 us
    all_gather x5, waiting for transfers between devices, gather(): return lax.all_gather(value, 'tensor', axis=1, tiled=True)  139 us
    dot_general x3, matrix products, contract_rows(): lax.dot_general(left, right, (((0,), (0,)), ((), ())), preferred_element_...  33.6 us
    dot_general x3, matrix products, project(): jnp.dot(left, right, preferred_element_type=jnp.float32)  32.8 us
    dot_general x3, matrix products, back_project(): lax.dot_general(left, right, (((1,), (1,)), ((), ())), preferred_element_...  31.6 us
    all_to_all x1, blocking collectives, body(): lax.all_to_all(send, 'expert', split_axis=0, concat_axis=0, tiled=True)  30.5 us
    psum x1, blocking collectives, body(): score = lax.psum(local_score, 'tensor')  13.4 us
  transfers between devices with their start and end apart: 10, of which 8 were waited for; matrix products, arithmetic and copies ran while one was open for 20% of the time, Pallas kernels for 0%

commit v1 on v0

--- a/solution.py
+++ b/solution.py
@@ -2,6 +2,18 @@
 import jax.numpy as jnp
 from jax import lax
 from jax.sharding import PartitionSpec as P
+
+
+def collect(array, axis, dim):
+    ways, here, turn = (lax.axis_size(axis), lax.axis_index(axis), array.shape[dim])
+    line, have = (array, 1)
+    while have < ways:
+        line = jnp.concatenate(
+            [line, lax.ppermute(line, axis, [(d, (d - have) % ways) for d in range(ways)])],
+            axis=dim,
+        )
+        have = 2 * have
+    return jnp.roll(line, here * turn, axis=dim)
 
 
 def gate_tables(expert_ids, route_logits, count):
@@ -59,7 +71,7 @@
         return full.astype(jnp.float32)
 
     def gather(value):
-        return lax.all_gather(value, "tensor", axis=1, tiled=True)
+        return collect(value, "tensor", 1)
 
     def back_project(left, right):
         return lax.dot_general(

time: 472 us -> 643 us (1.36); the launches traced: 472 us -> 635 us
  blocking collectives: 43.9 us -> 104 us
  matrix products: 102 us -> 131 us
  waiting for transfers between devices: 295 us -> 323 us
  other arithmetic: 6.8 us -> 33.2 us
  starting transfers between devices: 9.82 us -> 26.3 us
    ppermute x0 -> x15, waiting for transfers between devices: none -> 173 us  [collect(): lax.ppermute(line, axis, [(d, (d - have) % ways) for d in range(ways)])]
    all_gather x5 -> x0, waiting for transfers between devices: 139 us -> none  [gather(): return lax.all_gather(value, 'tensor', axis=1, tiled=True)]
    psum x1, blocking collectives: 13.4 us -> 73.9 us  [body(): score = lax.psum(local_score, 'tensor')]
    concatenate x0 -> x11, other arithmetic: none -> 27.5 us  [the longest x10 14.6 us: collect(): jnp.concatenate([line, lax.ppermute(line, axis, [(d, (d - have) % ways) f...]
    dot_general x3, matrix products: 31.6 us -> 56.5 us  [back_project(): lax.dot_general(left, right, (((1,), (1,)), ((), ())), preferred_element_...]
    ppermute x0 -> x15, starting transfers between devices: none -> 16.8 us  [collect(): lax.ppermute(line, axis, [(d, (d - have) % ways) for d in range(ways)])]
  transfers between devices with their start and end apart: 10 -> 20, of which waited for: 8 -> 10; matrix products, arithmetic and copies ran while one was open for 20% -> 24% of each run, Pallas kernels for 0% -> 0%
where the time goes in v1:
time: 643 us; the launch traced here: 635 us
  waiting for transfers between devices  323 us (50%)
  matrix products  131 us (20%)
  blocking collectives  104 us (16%)
  other arithmetic  33.2 us (5%)
  starting transfers between devices  26.3 us (4%)
  between operations  14.1 us (2%)
    ppermute x15, waiting for transfers between devices, collect(): lax.ppermute(line, axis, [(d, (d - have) % ways) for d in range(ways)])  173 us
    reduce_scatter x3, waiting for transfers between devices, project(): full = lax.psum_scatter(part, 'tensor', scatter_dimension=1, tiled=True)  149 us
    psum x1, blocking collectives, body(): score = lax.psum(local_score, 'tensor')  73.9 us
    dot_general x3, matrix products, back_project(): lax.dot_general(left, right, (((1,), (1,)), ((), ())), preferred_element_...  56.5 us
    dot_general x3, matrix products, contract_rows(): lax.dot_general(left, right, (((0,), (0,)), ((), ())), preferred_element_...  38.7 us
    dot_general x3, matrix products, project(): jnp.dot(left, right, preferred_element_type=jnp.float32)  32.3 us
    all_to_all x1, blocking collectives, body(): lax.all_to_all(send, 'expert', split_axis=0, concat_axis=0, tiled=True)  30.5 us
    ppermute x15, starting transfers between devices, collect(): lax.ppermute(line, axis, [(d, (d - have) % ways) for d in range(ways)])  16.8 us
  transfers between devices with their start and end apart: 20, of which 10 were waited for; matrix products, arithmetic and copies ran while one was open for 24% of the time, Pallas kernels for 0%

profile of v1, /device:TPU:0, one launch (start us, length us, event | category | flops | bytes accessed | tf_op | source)
XLA Modules:
  0.0 635.1 jit_solution(3140959229453547641)
XLA Ops:
  7.2 0.8 broadcast_subtract_fusion
  8.0 0.7 convert_reduce_fusion
  8.7 0.2 fusion.108
  8.9 1.0 convert_element_type.68
  9.9 0.3 fusion.82
  10.2 0.4 fusion.83
  10.6 0.1 pad_maximum_fusion.8
  10.7 0.1 copy.21
  10.7 30.5 %all_to_all.15 = bf16[4,2,80,768]{3,2,1,0:T(8,128)(2,1)S(1)} all-to-all(bf16[4,2,80,768]{3,2,1,0:T(8,128)(2,1)S(1)} %copy.21), channel_id=1, replica_groups=mesh['expert'=4,'tensor'=8] {'expert'}, dimensions={0} | all-to-all | bytes 1966080 | tf_op jit(solution)/shard_map/all_to_all | solution.py:63
  41.2 0.1 fusion.132
  41.3 10.5 %fusion.18 = bf16[320,8192]{1,0:T(8,128)(2,1)} fusion(bf16[320,768]{1,0:T(8,128)(2,1)S(1)} %bitcast.72, bf16[1,768,8192]{2,1,0:T(8,128)(2,1)} %param.20), kind=kOutput, calls=%fused_computation.17 | convolution fusion | flops 4029153280 | bytes 18317312 | tf_op jit(solution)/shard_map/dot_general | solution.py:69
  51.9 10.6 %fusion.15 = bf16[320,8192]{1,0:T(8,128)(2,1)} fusion(bf16[320,768]{1,0:T(8,128)(2,1)S(1)} %bitcast.66, bf16[1,768,8192]{2,1,0:T(8,128)(2,1)} %param.19), kind=kOutput, calls=%fused_computation.16 | convolution fusion | flops 4029153280 | bytes 18317312 | tf_op jit(solution)/shard_map/dot_general | solution.py:69
  62.5 11.2 %fusion.12 = bf16[320,8192]{1,0:T(8,128)(2,1)} fusion(bf16[320,768]{1,0:T(8,128)(2,1)S(1)} %bitcast.67, bf16[1,768,8192]{2,1,0:T(8,128)(2,1)} %param.18), kind=kOutput, calls=%fused_computation.15 | convolution fusion | flops 4029153280 | bytes 18317312 | tf_op jit(solution)/shard_map/dot_general | solution.py:69
  73.7 1.5 collective-permute-start.9
  75.2 17.0 %collective-permute-done.9 = bf16[320,768]{1,0:T(8,128)(2,1)S(1)} collective-permute-done((bf16[320,768]{1,0:T(8,128)(2,1)S(1)}, bf16[320,768]{1,0:T(8,128)(2,1)S(1)}, u32[]{:S(2)}, u32[]{:S(2)}) %collective-permute-start.9) | collective-permute-done | bytes 491552 | tf_op jit(solution)/shard_map/ppermute | solution.py:12
  92.3 0.8 collective-permute-start.10
  93.2 2.2 collective-permute-start.12
  95.3 25.3 %collective-permute-done.12 = bf16[320,768]{1,0:T(8,128)(2,1)S(1)} collective-permute-done((bf16[320,768]{1,0:T(8,128)(2,1)S(1)}, bf16[320,768]{1,0:T(8,128)(2,1)S(1)}, u32[]{:S(2)}, u32[]{:S(2)}) %collective-permute-start.12) | collective-permute-done | bytes 491552 | tf_op jit(solution)/shard_map/ppermute | solution.py:12
  120.7 1.7 collective-permute-start.13
  122.3 1.0 copy-done.3
  123.3 1.5 pad_maximum_fusion.3
  124.8 0.6 collective-permute-start.11
  125.4 26.8 %collective-permute-done.13 = bf16[320,1536]{1,0:T(8,128)(2,1)S(1)} collective-permute-done((bf16[320,1536]{1,0:T(8,128)(2,1)S(1)}, bf16[320,1536]{1,0:T(8,128)(2,1)S(1)}, u32[]{:S(2)}, u32[]{:S(2)}) %collective-permute-start.13) | collective-permute-done | bytes 983072 | tf_op jit(solution)/shard_map/ppermute | solution.py:12
  152.3 1.6 pad_maximum_fusion.4
  153.9 88.3 %reduce-scatter.6.cloned.1.call-done = bf16[320,1024]{1,0:T(8,128)(2,1)} async-done(((bf16[320,8192]{1,0:T(8,128)(2,1)}), bf16[320,1024]{1,0:T(8,128)(2,1)}) %reduce-scatter.6.cloned.1.call-update) | async-done | bytes 655376 | tf_op jit(solution)/shard_map/reduce_scatter | solution.py:70
  242.3 61.0 %reduce-scatter.4.cloned.1.call-done = bf16[320,1024]{1,0:T(8,128)(2,1)} async-done(((bf16[320,8192]{1,0:T(8,128)(2,1)}), bf16[320,1024]{1,0:T(8,128)(2,1)}) %reduce-scatter.4.cloned.1.call-update) | async-done | bytes 655376 | tf_op jit(solution)/shard_map/reduce_scatter | solution.py:70
  303.2 2.5 multiply_convert_fusion.2
  305.8 1.0 collective-permute-start
  306.7 12.9 %fusion.60 = bf16[320,6144]{1,0:T(8,128)(2,1)} fusion(s32[]{:T(128)S(6)} %select_n.40, bf16[320,768]{1,0:T(8,128)(2,1)S(1)} %bitcast.71, bf16[320,768]{1,0:T(8,128)(2,1)S(1)} %collective-permute-done.9, bf16[320,1536]{1,0:T(8,128)(2,1)} %copy-done.3, bf16[320,3072]{1,0:T(8,128)(2,1)} %collective-permute-done.11), kind=kLoop, calls=%fused_computation.89 | loop fusion | flops 31457280 | bytes 7864324 | tf_op jit(solution)/shard_map/jit(_roll_dynamic)/concatenate | solution.py:16
  319.7 0.8 collective-permute-start.3
  320.5 0.8 collective-permute-start.6
  321.3 0.8 copy-done.4
  322.1 1.2 pad_maximum_fusion.5
  323.3 1.4 collective-permute-start.1
  324.7 19.3 %convert_bitcast_fusion = bf16[1,6144,1024]{2,1,0:T(8,128)(2,1)} fusion(bf16[320,1024]{1,0:T(8,128)(2,1)S(1)} %get-tuple-element.13, s32[]{:T(128)S(6)} %select_n.40, bf16[320,768]{1,0:T(8,128)(2,1)S(1)} %bitcast.76, bf16[320,768]{1,0:T(8,128)(2,1)} %copy-done.6, bf16[320,1536]{1,0:T(8,128)(2,1)} %copy-done.9, bf16[320,3072]{1,0:T(8,128)(2,1)} %collective-permute-done.14), kind=kOutput, calls=%fused_computation.12 | convolution fusion | flops 4064280576 | bytes 17170436 | tf_op jit(solution)/shard_map/dot_general | solution.py:30
  344.0 20.9 %collective-permute-done.1 = bf16[320,2048]{1,0:T(8,128)(2,1)} collective-permute-done((bf16[320,2048]{1,0:T(8,128)(2,1)}, bf16[320,2048]{1,0:T(8,128)(2,1)}, u32[]{:S(2)}, u32[]{:S(2)}) %collective-permute-start.1) | collective-permute-done | bytes 1310752 | tf_op jit(solution)/shard_map/ppermute | solution.py:12
  364.9 1.7 pad_maximum_fusion
  366.6 1.5 collective-permute-start.2
  368.1 9.7 %convert_bitcast_fusion.2 = bf16[1,6144,1024]{2,1,0:T(8,128)(2,1)} fusion(bf16[320,6144]{1,0:T(8,128)(2,1)S(1)} %copy-done.2, bf16[320,1024]{1,0:T(8,128)(2,1)S(1)} %get-tuple-element.12), kind=kOutput, calls=%fused_computation.14 | convolution fusion | flops 4032823296 | bytes 17170432 | tf_op jit(solution)/shard_map/dot_general | solution.py:30
  377.8 1.2 pad_maximum_fusion.7
  379.0 2.4 collective-permute-start.7
  381.4 1.2 pad_maximum_fusion.6
  382.6 0.5 collective-permute-start.4
  383.1 9.7 %convert_bitcast_fusion.1 = bf16[1,6144,1024]{2,1,0:T(8,128)(2,1)} fusion(bf16[320,6144]{1,0:T(8,128)(2,1)S(1)} %copy-done.2, bf16[320,1024]{1,0:T(8,128)(2,1)S(1)} %get-tuple-element.14), kind=kOutput, calls=%fused_computation.13 | convolution fusion | flops 4032823296 | bytes 17170432 | tf_op jit(solution)/shard_map/dot_general | solution.py:30
  392.8 17.9 %collective-permute-done.7 = bf16[320,2048]{1,0:T(8,128)(2,1)S(1)} collective-permute-done((bf16[320,2048]{1,0:T(8,128)(2,1)S(1)}, bf16[320,2048]{1,0:T(8,128)(2,1)S(1)}, u32[]{:S(2)}, u32[]{:S(2)}) %collective-permute-start.7) | collective-permute-done | bytes 1310752 | tf_op jit(solution)/shard_map/ppermute | solution.py:12
  410.7 3.3 pad_maximum_fusion.2
  414.0 0.9 collective-permute-start.8
  414.9 11.8 %collective-permute-done.4 = bf16[320,2048]{1,0:T(8,128)(2,1)S(1)} collective-permute-done((bf16[320,2048]{1,0:T(8,128)(2,1)S(1)}, bf16[320,2048]{1,0:T(8,128)(2,1)S(1)}, u32[]{:S(2)}, u32[]{:S(2)}) %collective-permute-start.4) | collective-permute-done | bytes 1310752 | tf_op jit(solution)/shard_map/ppermute | solution.py:12
  426.7 1.1 copy-done.7
  427.8 2.8 pad_maximum_fusion.1
  430.6 0.6 collective-permute-start.5
  431.2 18.8 %fusion.77 = bf16[320,768]{1,0:T(8,128)(2,1)} fusion(bf16[1,768,8192]{2,1,0:T(8,128)(2,1)} %param.20, s32[]{:T(128)S(6)} %select_n.34, bf16[320,1024]{1,0:T(8,128)(2,1)S(1)} %get-tuple-element.13, bf16[320,1024]{1,0:T(8,128)(2,1)S(1)} %copy-done.5, bf16[320,2048]{1,0:T(8,128)(2,1)} %collective-permute-done.1, bf16[320,4096]{1,0:T(8,128)(2,1)} %collective-permute-done.2), kind=kOutput, calls=%fused_computation.117 | convolution fusion | flops 4068720640 | bytes 18317316 | tf_op jit(solution)/shard_map/dot_general | solution.py:77
  449.9 4.8 all-to-all-start.1
  454.7 28.0 %collective-permute-done.8 = bf16[320,4096]{1,0:T(8,128)(2,1)} collective-permute-done((bf16[320,4096]{1,0:T(8,128)(2,1)}, bf16[320,4096]{1,0:T(8,128)(2,1)}, u32[]{:S(2)}, u32[]{:S(2)}) %collective-permute-start.8) | collective-permute-done | bytes 2621472 | tf_op jit(solution)/shard_map/ppermute | solution.py:12
  482.7 18.8 %fusion.4 = f32[320,768]{1,0:T(8,128)} fusion(bf16[1,768,8192]{2,1,0:T(8,128)(2,1)} %param.19, s32[]{:T(128)S(6)} %select_n.34, bf16[320,1024]{1,0:T(8,128)(2,1)S(1)} %get-tuple-element.14, bf16[320,1024]{1,0:T(8,128)(2,1)} %collective-permute-done.6, bf16[320,2048]{1,0:T(8,128)(2,1)} %copy-done.8, bf16[320,4096]{1,0:T(8,128)(2,1)} %collective-permute-done.8), kind=kOutput, calls=%fused_computation.4 | convolution fusion | flops 4068474880 | bytes 18808836 | tf_op jit(solution)/shard_map/dot_general | solution.py:77
  501.5 25.6 %collective-permute-done.5 = bf16[320,4096]{1,0:T(8,128)(2,1)} collective-permute-done((bf16[320,4096]{1,0:T(8,128)(2,1)}, bf16[320,4096]{1,0:T(8,128)(2,1)}, u32[]{:S(2)}, u32[]{:S(2)}) %collective-permute-start.5) | collective-permute-done | bytes 2621472 | tf_op jit(solution)/shard_map/ppermute | solution.py:12
  527.1 18.9 %fusion.72 = bf16[320,768]{1,0:T(8,128)(2,1)} fusion(f32[320,768]{1,0:T(8,128)} %fusion.4, bf16[1,768,8192]{2,1,0:T(8,128)(2,1)} %param.18, s32[]{:T(128)S(6)} %select_n.34, bf16[320,1024]{1,0:T(8,128)(2,1)S(1)} %get-tuple-element.12, bf16[320,1024]{1,0:T(8,128)(2,1)} %collective-permute-done.3, bf16[320,2048]{1,0:T(8,128)(2,1)} %copy-done.7, ...), kind=kOutput, calls=%fused_computation.116 | convolution fusion | flops 4068966400 | bytes 19300356 | tf_op jit(solution)/shard_map/dot_general | solution.py:77
  546.0 4.6 all-to-all-start.2
  550.6 1.1 multiply_reduce_fusion
  551.7 1.0 fusion.64
  552.8 0.1 copy.24
  552.8 73.9 %psum.7 = f32[128,4]{0,1:T(4,128)S(1)} all-reduce(f32[128,4]{0,1:T(4,128)S(1)} %bitcast.81), channel_id=1, replica_groups=mesh['expert'=4,'tensor'=8] {'tensor'}, use_global_device_ids=true, to_apply=%region_6.8 | all-reduce | flops 512 | bytes 4096 | tf_op jit(solution)/shard_map/psum | solution.py:116
  626.8 0.6 subtract_multiply_fusion
  627.4 1.0 fusion.84
  (51 shorter events, 0.5 us)
Async XLA Ops:
  7.2 2.7 copy-start
  7.2 146.8 %reduce-scatter.8.cloned.1.call-start = ((), (), s32[]{:S(2)}) async-start(), calls=%async_computation.8 | async-start | bytes 5898240 | tf_op jit(solution)/shard_map/reduce_scatter | solution.py:70
  51.8 190.4 %reduce-scatter.6.cloned.1.call-start = ((), (), s32[]{:S(2)}) async-start(), calls=%async_computation.7 | async-start | bytes 5898240 | tf_op jit(solution)/shard_map/reduce_scatter | solution.py:70
  62.5 240.8 %reduce-scatter.4.cloned.1.call-start = ((), (), s32[]{:S(2)}) async-start(), calls=%async_computation.6 | async-start | bytes 5898240 | tf_op jit(solution)/shard_map/reduce_scatter | solution.py:70
  73.7 18.5 %collective-permute-start.9 = (bf16[320,768]{1,0:T(8,128)(2,1)S(1)}, bf16[320,768]{1,0:T(8,128)(2,1)S(1)}, u32[]{:S(2)}, u32[]{:S(2)}) collective-permute-start(bf16[320,768]{1,0:T(8,128)(2,1)S(1)} %bitcast.68), channel_id=1, source_target_pairs={{0,7},{1,0},{2,1},{3,2},{4,3},{5,4},{6,5},{7,6},{8,15},{9,8},{10,9... | collective-permute-start | bytes 1474568 | tf_op jit(solution)/shard_map/ppermute | solution.py:12
  92.3 210.9 %copy-start.11 = (f32[1,1024]{1,0:T(1,128)S(1)}, f32[1,1024]{1,0:T(1,128)}, u32[]{:S(2)}) copy-start(f32[1,1024]{1,0:T(1,128)} %param.23) | copy-start | bytes 12292
  92.3 210.9 %copy-start.12 = (f32[1,1024]{1,0:T(1,128)S(1)}, f32[1,1024]{1,0:T(1,128)}, u32[]{:S(2)}) copy-start(f32[1,1024]{1,0:T(1,128)} %param.22) | copy-start | bytes 12292
  92.3 210.9 %copy-start.13 = (f32[1,1024]{1,0:T(1,128)S(1)}, f32[1,1024]{1,0:T(1,128)}, u32[]{:S(2)}) copy-start(f32[1,1024]{1,0:T(1,128)} %param.21) | copy-start | bytes 12292
  92.3 30.0 %collective-permute-start.10 = (bf16[320,1536]{1,0:T(8,128)(2,1)S(1)}, bf16[320,1536]{1,0:T(8,128)(2,1)S(1)}, u32[]{:S(2)}, u32[]{:S(2)}) collective-permute-start(bf16[320,1536]{1,0:T(8,128)(2,1)S(1)} %pad_maximum_fusion.9), channel_id=1, source_target_pairs={{0,6},{1,7},{2,0},{3,1},{4,2},{5,3},{6,4},{7,5},{8,14},{9,15},{10,... | collective-permute-start | bytes 2949128 | tf_op jit(solution)/shard_map/ppermute | solution.py:12
  93.2 27.4 %collective-permute-start.12 = (bf16[320,768]{1,0:T(8,128)(2,1)S(1)}, bf16[320,768]{1,0:T(8,128)(2,1)S(1)}, u32[]{:S(2)}, u32[]{:S(2)}) collective-permute-start(bf16[320,768]{1,0:T(8,128)(2,1)S(1)} %bitcast.73), channel_id=1, source_target_pairs={{0,7},{1,0},{2,1},{3,2},{4,3},{5,4},{6,5},{7,6},{8,15},{9,8},{10,9... | collective-permute-start | bytes 1474568 | tf_op jit(solution)/shard_map/ppermute | solution.py:12
  120.6 31.7 %copy-start.6 = (bf16[320,768]{1,0:T(8,128)(2,1)}, bf16[320,768]{1,0:T(8,128)(2,1)S(1)}, u32[]{:S(2)}) copy-start(bf16[320,768]{1,0:T(8,128)(2,1)S(1)} %collective-permute-done.12) | copy-start | bytes 1474564
  120.7 31.6 %collective-permute-start.13 = (bf16[320,1536]{1,0:T(8,128)(2,1)S(1)}, bf16[320,1536]{1,0:T(8,128)(2,1)S(1)}, u32[]{:S(2)}, u32[]{:S(2)}) collective-permute-start(bf16[320,1536]{1,0:T(8,128)(2,1)S(1)} %pad_maximum_fusion.10), channel_id=1, source_target_pairs={{0,6},{1,7},{2,0},{3,1},{4,2},{5,3},{6,4},{7,5},{8,14},{9,15},{10,... | collective-permute-start | bytes 2949128 | tf_op jit(solution)/shard_map/ppermute | solution.py:12
  122.3 1.0 copy-start.3
  124.8 181.9 %collective-permute-start.11 = (bf16[320,3072]{1,0:T(8,128)(2,1)}, bf16[320,3072]{1,0:T(8,128)(2,1)}, u32[]{:S(2)}, u32[]{:S(2)}) collective-permute-start(bf16[320,3072]{1,0:T(8,128)(2,1)} %pad_maximum_fusion.3), channel_id=1, source_target_pairs={{0,4},{1,5},{2,6},{3,7},{4,0},{5,1},{6,2},{7,3},{8,12},{9,13},{10,... | collective-permute-start | bytes 5898248 | tf_op jit(solution)/shard_map/ppermute | solution.py:12
  152.3 1.6 copy-start.9
  153.9 170.8 %collective-permute-start.14 = (bf16[320,3072]{1,0:T(8,128)(2,1)}, bf16[320,3072]{1,0:T(8,128)(2,1)}, u32[]{:S(2)}, u32[]{:S(2)}) collective-permute-start(bf16[320,3072]{1,0:T(8,128)(2,1)} %pad_maximum_fusion.4), channel_id=1, source_target_pairs={{0,4},{1,5},{2,6},{3,7},{4,0},{5,1},{6,2},{7,3},{8,12},{9,13},{10,... | collective-permute-start | bytes 5898248 | tf_op jit(solution)/shard_map/ppermute | solution.py:12
  305.8 15.5 %collective-permute-start = (bf16[320,1024]{1,0:T(8,128)(2,1)S(1)}, bf16[320,1024]{1,0:T(8,128)(2,1)S(1)}, u32[]{:S(2)}, u32[]{:S(2)}) collective-permute-start(bf16[320,1024]{1,0:T(8,128)(2,1)S(1)} %get-tuple-element.13), channel_id=1, source_target_pairs={{0,7},{1,0},{2,1},{3,2},{4,3},{5,4},{6,5},{7,6},{8,15},{9,8},{10,9... | collective-permute-start | bytes 1966088 | tf_op jit(solution)/shard_map/ppermute | solution.py:12
  319.7 61.8 %collective-permute-start.3 = (bf16[320,1024]{1,0:T(8,128)(2,1)S(1)}, bf16[320,1024]{1,0:T(8,128)(2,1)}, u32[]{:S(2)}, u32[]{:S(2)}) collective-permute-start(bf16[320,1024]{1,0:T(8,128)(2,1)S(1)} %get-tuple-element.12), channel_id=1, source_target_pairs={{0,7},{1,0},{2,1},{3,2},{4,3},{5,4},{6,5},{7,6},{8,15},{9,8},{10,9... | collective-permute-start | bytes 1966088 | tf_op jit(solution)/shard_map/ppermute | solution.py:12
  320.5 57.3 %collective-permute-start.6 = (bf16[320,1024]{1,0:T(8,128)(2,1)S(1)}, bf16[320,1024]{1,0:T(8,128)(2,1)}, u32[]{:S(2)}, u32[]{:S(2)}) collective-permute-start(bf16[320,1024]{1,0:T(8,128)(2,1)S(1)} %get-tuple-element.14), channel_id=1, source_target_pairs={{0,7},{1,0},{2,1},{3,2},{4,3},{5,4},{6,5},{7,6},{8,15},{9,8},{10,9... | collective-permute-start | bytes 1966088 | tf_op jit(solution)/shard_map/ppermute | solution.py:12
  321.3 0.8 copy-start.4
  323.3 41.6 %collective-permute-start.1 = (bf16[320,2048]{1,0:T(8,128)(2,1)}, bf16[320,2048]{1,0:T(8,128)(2,1)}, u32[]{:S(2)}, u32[]{:S(2)}) collective-permute-start(bf16[320,2048]{1,0:T(8,128)(2,1)} %pad_maximum_fusion.5), channel_id=1, source_target_pairs={{0,6},{1,7},{2,0},{3,1},{4,2},{5,3},{6,4},{7,5},{8,14},{9,15},{10,... | collective-permute-start | bytes 3932168 | tf_op jit(solution)/shard_map/ppermute | solution.py:12
  344.0 24.1 %copy-start.2 = (bf16[320,6144]{1,0:T(8,128)(2,1)S(1)}, bf16[320,6144]{1,0:T(8,128)(2,1)}, u32[]{:S(2)}) copy-start(bf16[320,6144]{1,0:T(8,128)(2,1)} %fusion.60) | copy-start | bytes 11796484
  366.6 64.6 %collective-permute-start.2 = (bf16[320,4096]{1,0:T(8,128)(2,1)S(1)}, bf16[320,4096]{1,0:T(8,128)(2,1)}, u32[]{:S(2)}, u32[]{:S(2)}) collective-permute-start(bf16[320,4096]{1,0:T(8,128)(2,1)S(1)} %pad_maximum_fusion), channel_id=1, source_target_pairs={{0,4},{1,5},{2,6},{3,7},{4,0},{5,1},{6,2},{7,3},{8,12},{9,13},{10,... | collective-permute-start | bytes 7864328 | tf_op jit(solution)/shard_map/ppermute | solution.py:12
  379.0 31.7 %collective-permute-start.7 = (bf16[320,2048]{1,0:T(8,128)(2,1)S(1)}, bf16[320,2048]{1,0:T(8,128)(2,1)S(1)}, u32[]{:S(2)}, u32[]{:S(2)}) collective-permute-start(bf16[320,2048]{1,0:T(8,128)(2,1)S(1)} %pad_maximum_fusion.7), channel_id=1, source_target_pairs={{0,6},{1,7},{2,0},{3,1},{4,2},{5,3},{6,4},{7,5},{8,14},{9,15},{10,... | collective-permute-start | bytes 3932168 | tf_op jit(solution)/shard_map/ppermute | solution.py:12
  382.6 44.1 %collective-permute-start.4 = (bf16[320,2048]{1,0:T(8,128)(2,1)S(1)}, bf16[320,2048]{1,0:T(8,128)(2,1)S(1)}, u32[]{:S(2)}, u32[]{:S(2)}) collective-permute-start(bf16[320,2048]{1,0:T(8,128)(2,1)S(1)} %pad_maximum_fusion.6), channel_id=1, source_target_pairs={{0,6},{1,7},{2,0},{3,1},{4,2},{5,3},{6,4},{7,5},{8,14},{9,15},{10,... | collective-permute-start | bytes 3932168 | tf_op jit(solution)/shard_map/ppermute | solution.py:12
  392.8 38.4 %copy-start.5 = (bf16[320,1024]{1,0:T(8,128)(2,1)S(1)}, bf16[320,1024]{1,0:T(8,128)(2,1)}, u32[]{:S(2)}) copy-start(bf16[320,1024]{1,0:T(8,128)(2,1)} %copy-done.4) | copy-start | bytes 1966084
  410.7 19.9 %copy-start.8 = (bf16[320,2048]{1,0:T(8,128)(2,1)}, bf16[320,2048]{1,0:T(8,128)(2,1)S(1)}, u32[]{:S(2)}) copy-start(bf16[320,2048]{1,0:T(8,128)(2,1)S(1)} %collective-permute-done.7) | copy-start | bytes 3932164
  414.0 68.6 %collective-permute-start.8 = (bf16[320,4096]{1,0:T(8,128)(2,1)}, bf16[320,4096]{1,0:T(8,128)(2,1)}, u32[]{:S(2)}, u32[]{:S(2)}) collective-permute-start(bf16[320,4096]{1,0:T(8,128)(2,1)} %pad_maximum_fusion.2), channel_id=1, source_target_pairs={{0,4},{1,5},{2,6},{3,7},{4,0},{5,1},{6,2},{7,3},{8,12},{9,13},{10,... | collective-permute-start | bytes 7864328 | tf_op jit(solution)/shard_map/ppermute | solution.py:12
  426.7 1.1 copy-start.7
  430.6 96.5 %collective-permute-start.5 = (bf16[320,4096]{1,0:T(8,128)(2,1)}, bf16[320,4096]{1,0:T(8,128)(2,1)}, u32[]{:S(2)}, u32[]{:S(2)}) collective-permute-start(bf16[320,4096]{1,0:T(8,128)(2,1)} %pad_maximum_fusion.1), channel_id=1, source_target_pairs={{0,4},{1,5},{2,6},{3,7},{4,0},{5,1},{6,2},{7,3},{8,12},{9,13},{10,... | collective-permute-start | bytes 7864328 | tf_op jit(solution)/shard_map/ppermute | solution.py:12
  449.9 96.1 %all-to-all-start.1 = ((bf16[4,80,768]{2,1,0:T(8,128)(2,1)}), bf16[4,80,768]{2,1,0:T(8,128)(2,1)S(1)}, u32[]{:S(2)}, u32[]{:S(2)}) async-start(bf16[4,80,768]{2,1,0:T(8,128)(2,1)} %bitcast.77), calls=%async_computation.3 | async-start | bytes 983040 | tf_op jit(solution)/shard_map/all_to_all | solution.py:82
  501.5 50.2 %copy-start.10 = (bf16[128,768]{1,0:T(8,128)(2,1)S(1)}, bf16[128,768]{1,0:T(8,128)(2,1)}, u32[]{:S(2)}) copy-start(bf16[128,768]{1,0:T(8,128)(2,1)} %param.15) | copy-start | bytes 589828
  527.1 101.3 %copy-start.1 = (bf16[128,768]{1,0:T(8,128)(2,1)S(1)}, bf16[128,768]{1,0:T(8,128)(2,1)}, u32[]{:S(2)}) copy-start(bf16[128,768]{1,0:T(8,128)(2,1)} %param.14) | copy-start | bytes 589828
  546.0 80.7 %copy-start.14 = (s32[128,2]{0,1:T(2,128)S(1)}, s32[128,2]{0,1:T(2,128)}, u32[]{:S(2)}) copy-start(s32[128,2]{0,1:T(2,128)} %param.16) | copy-start | bytes 3076
  546.0 81.4 %all-to-all-start.2 = ((bf16[4,80,768]{2,1,0:T(8,128)(2,1)}), bf16[4,80,768]{2,1,0:T(8,128)(2,1)S(1)}, u32[]{:S(2)}, u32[]{:S(2)}) async-start(bf16[4,80,768]{2,1,0:T(8,128)(2,1)} %bitcast.14), calls=%async_computation.5 | async-start | bytes 983040 | tf_op jit(solution)/shard_map/all_to_all | solution.py:82
Sparse Core Ops, SparseCore 0:
  52.0 94.1 reduce-scatter.7
  150.1 92.0 reduce-scatter.5
  246.2 56.9 reduce-scatter.3
